TPU v7x, 512 devices: a whole 4x8x8 slice. The times are simulated.
512 devices in a mesh: rep: 4 (over z_hi), dp: 16 (over y, core), tensor: 8 (over x, z_lo).
Axes of the slice: x: 4, y: 8, z: 8 (z_hi: 4, z_lo: 2; z = z_hi * 2 + z_lo), core: 2. Of those that a mesh axis runs over, the one named last changes fastest.
Arguments:
- grad_proj: float32 [64, 3072, 1536], P(('rep', 'dp'), 'tensor'), as said below
- grad_conv: float32 [64, 4, 3328], P(('rep', 'dp'), None, 'tensor'), may hold values from -24 to 24
- param_proj: float32 [3072, 1536], P('tensor', 'dp'), may hold values from -6 to 6
- m_proj: float32 [3072, 1536], P('tensor', 'dp'), may hold values from -2 to 2
- v_proj: float32 [3072, 1536], P('tensor', 'dp'), may hold values from 0.02 to 0.2
- ema_proj: float32 [3072, 1536], P(('tensor', 'dp')), may hold values from -6 to 6
- param_conv: float32 [4, 3328], P(None, 'tensor'), may hold values from -3 to 3
- m_conv: float32 [4, 3328], P(None, 'tensor'), may hold values from -2 to 2
- v_conv: float32 [4, 3328], P(None, 'tensor'), may hold values from 0.02 to 0.2
Outputs:
- new_param_proj: float32 [3072, 1536], P('tensor', 'dp')
- new_m_proj: float32 [3072, 1536], P('tensor', 'dp')
- new_v_proj: float32 [3072, 1536], P('tensor', 'dp')
- new_ema_proj: float32 [3072, 1536], P(('tensor', 'dp'))
- weights_proj: bfloat16 [3072, 1536], P('tensor')
- new_param_conv: float32 [4, 3328], P(None, 'tensor')
- new_m_conv: float32 [4, 3328], P(None, 'tensor')
- new_v_conv: float32 [4, 3328], P(None, 'tensor')
Inputs may be any that keep to these rules, and one draw needn't show every extreme that they name: `grad_proj`: Real-valued gradients with entries of magnitude below 3100.
All inputs are finite; a program needn't handle non-finite values.
Results may differ from a plain program's by a relative error of at most 0.001.
Values may be sent and summed in bfloat16 or wider, within the bound.
A program may use at most 64 MiB of HBM per device.

v0:
```python
import math
import jax
import jax.numpy as jnp
from jax import lax
from jax.sharding import PartitionSpec as P

D = 1536
INNER = 3072
CONV = 3328
KCONV = 4


def adamw_step(param_in, first_in, second_in, grad_in):
    first_out = 0.9 * first_in + 0.1 * grad_in
    second_out = 0.95 * second_in + 0.05 * grad_in * grad_in
    bias_one = 1.0 - 0.9**10
    bias_two = 1.0 - 0.95**10
    update = first_out / bias_one / (jnp.sqrt(second_out / bias_two) + 1e-08)
    param_out = param_in - 0.25 * (update + 0.1 * param_in)
    return (param_out, first_out, second_out)


def clip_from(square_sum):
    clip_limit = 0.5 * math.sqrt(INNER * D + KCONV * CONV)
    return jnp.minimum(1.0, clip_limit / (jnp.sqrt(square_sum) + 1e-06))


def body(grad_proj, grad_conv, param_proj, m_proj, v_proj, ema_proj, param_conv, m_conv, v_conv):
    replica_count = lax.axis_size("rep") * lax.axis_size("dp")
    conv_avg = lax.psum(grad_conv[0], ("rep", "dp")) / replica_count
    conv_square = jnp.sum(conv_avg * conv_avg)
    first_owner = lax.axis_index("dp") == 0
    owner_sum = lax.psum_scatter(grad_proj[0], "dp", scatter_dimension=1, tiled=True)
    proj_avg = lax.psum(owner_sum, "rep") / replica_count
    conv_share = jnp.where(first_owner, conv_square, jnp.float32(0.0))
    square_sum = lax.psum(jnp.sum(proj_avg * proj_avg) + conv_share, ("dp", "tensor"))
    clip_factor = clip_from(square_sum)
    new_param_proj, new_m_proj, new_v_proj = adamw_step(
        param_proj, m_proj, v_proj, clip_factor * proj_avg
    )
    new_param_conv, new_m_conv, new_v_conv = adamw_step(
        param_conv, m_conv, v_conv, clip_factor * conv_avg
    )
    ema_count = ema_proj.shape[0]
    full_block = lax.all_gather(
        new_param_proj.astype(jnp.bfloat16), "dp", axis=1, tiled=True
    ).astype(new_param_proj.dtype)
    weights_proj = full_block.astype(jnp.bfloat16)
    row_block = lax.dynamic_slice_in_dim(full_block, lax.axis_index("dp") * ema_count, ema_count, 0)
    new_ema_proj = 0.9 * ema_proj + 0.1 * row_block
    return (
        new_param_proj,
        new_m_proj,
        new_v_proj,
        new_ema_proj,
        weights_proj,
        new_param_conv,
        new_m_conv,
        new_v_conv,
    )


def solution(mesh):
    in_specs = (
        P(("rep", "dp"), "tensor", None),
        P(("rep", "dp"), None, "tensor"),
        P("tensor", "dp"),
        P("tensor", "dp"),
        P("tensor", "dp"),
        P(("tensor", "dp"), None),
        P(None, "tensor"),
        P(None, "tensor"),
        P(None, "tensor"),
    )
    out_specs = (
        P("tensor", "dp"),
        P("tensor", "dp"),
        P("tensor", "dp"),
        P(("tensor", "dp"), None),
        P("tensor", None),
        P(None, "tensor"),
        P(None, "tensor"),
        P(None, "tensor"),
    )
    return jax.shard_map(body, mesh=mesh, in_specs=in_specs, out_specs=out_specs, check_vma=False)
```

profile of v0, /device:TPU:1, one launch (start us, length us, event | category | flops | bytes accessed | tf_op | source)
XLA Modules:
  0.0 549.1 jit_solution(13845586338401462347)
XLA Ops:
  7.2 0.0 reduce-scatter.2.cloned.1.call-start
  7.2 3.1 copy.19
  10.3 0.0 copy-start.8
  10.3 0.0 copy-start.2
  10.3 0.0 copy-start.3
  10.3 0.0 copy-start.4
  10.3 0.0 reduce-scatter.2.cloned.1.call-update
  10.3 0.0 copy-start.1
  10.3 0.0 all-reduce.2.cloned.1.call-start
  10.4 66.1 %reduce-scatter.2.cloned.1.call-done = f32[384,96]{0,1:T(8,128)} async-done(((f32[384,1536]{0,1:T(8,128)}), f32[384,96]{0,1:T(8,128)}) %reduce-scatter.2.cloned.1.call-update) | async-done | bytes 147472 | tf_op jit(solution)/shard_map/reduce_scatter | solution.py:33
  76.5 0.0 all-reduce.2.cloned.1.call-update
  76.5 0.0 copy-start.5
  76.5 0.0 copy-start.6
  76.5 0.0 copy-start.7
  76.5 0.0 all-gather.2.cloned.1.call-start
  76.6 0.0 copy-done.8
  76.6 142.5 %psum.22 = f32[4,416]{1,0:T(4,128)S(1)} all-reduce(f32[4,416]{1,0:T(4,128)S(1)} %bitcast.3), channel_id=1, replica_groups=mesh['rep'=4,'dp'=16,'tensor'=8] {'rep','dp'}, use_global_device_ids=true, to_apply=%region_3.0 | all-reduce | flops 1664 | bytes 13312 | tf_op jit(solution)/shard_map/psum | solution.py:30
  219.1 0.6 multiply_reduce_fusion.1
  220.3 0.0 all-reduce.2.cloned.1.call-done
  220.4 1.6 multiply_reduce_fusion
  222.6 270.7 %psum.23 = f32[]{:T(128)} all-reduce(f32[]{:T(128)S(6)} %add.50), channel_id=1, replica_groups=mesh['rep'=4,'dp'=16,'tensor'=8] {'dp','tensor'}, use_global_device_ids=true, to_apply=%region_5.6 | all-reduce | flops 1 | bytes 8 | tf_op jit(solution)/shard_map/psum | solution.py:36
  494.0 0.0 copy-done.2
  494.0 0.0 copy-done.3
  494.0 0.0 copy-done.4
  494.0 1.8 fusion.3
  495.7 0.0 all-gather.2.cloned.1.call-update
  495.8 0.0 copy-done.1
  495.8 0.3 copy.20
  496.1 0.0 copy-done.5
  496.1 0.0 copy-done.6
  496.1 0.0 copy-done.7
  496.1 0.6 multiply_subtract_fusion.1
  496.7 42.1 %all-gather.2.cloned.1.call-done = bf16[384,1536]{0,1:T(8,128)(2,1)} async-done(((bf16[384,96]{0,1:T(8,128)(2,1)}), bf16[384,1536]{0,1:T(8,128)(2,1)}) %all-gather.2.cloned.1.call-update) | async-done | bytes 1179664 | tf_op jit(solution)/shard_map/all_gather | solution.py:45
  538.8 0.0 copy-start
  538.8 1.4 multiply_add_fusion
  540.3 0.9 copy.21
  541.2 0.0 copy-done
  541.2 1.4 copy.22
Async XLA Ops:
  7.2 69.3 %reduce-scatter.2.cloned.1.call-start = ((), (), s32[]{:S(2)}) async-start(), calls=%async_computation.1 | async-start | bytes 2506752 | tf_op jit(solution)/shard_map/reduce_scatter | solution.py:33
  10.3 66.3 %copy-start.8 = (f32[1,4,416]{2,1,0:T(4,128)S(1)}, f32[1,4,416]{2,1,0:T(4,128)}, u32[]{:S(2)}) copy-start(f32[1,4,416]{2,1,0:T(4,128)} %param.10) | copy-start | bytes 19972
  10.3 483.7 %copy-start.2 = (f32[384,96]{0,1:T(8,128)S(1)}, f32[384,96]{0,1:T(8,128)}, u32[]{:S(2)}) copy-start(f32[384,96]{0,1:T(8,128)} %param.11) | copy-start | bytes 442372
  10.3 483.7 %copy-start.3 = (f32[384,96]{0,1:T(8,128)S(1)}, f32[384,96]{0,1:T(8,128)}, u32[]{:S(2)}) copy-start(f32[384,96]{0,1:T(8,128)} %param.12) | copy-start | bytes 442372
  10.3 483.7 %copy-start.4 = (f32[384,96]{0,1:T(8,128)S(1)}, f32[384,96]{0,1:T(8,128)}, u32[]{:S(2)}) copy-start(f32[384,96]{0,1:T(8,128)} %param.13) | copy-start | bytes 442372
  10.3 485.4 %copy-start.1 = (f32[24,1536]{1,0:T(8,128)S(1)}, f32[24,1536]{1,0:T(8,128)}, u32[]{:S(2)}) copy-start(f32[24,1536]{1,0:T(8,128)} %param.14) | copy-start | bytes 442372
  10.3 210.0 %all-reduce.2.cloned.1.call-start = ((), (), s32[]{:S(2)}) async-start(), calls=%async_computation.2 | async-start | bytes 294912 | tf_op jit(solution)/shard_map/psum | solution.py:34
  76.5 419.6 %copy-start.5 = (f32[4,416]{1,0:T(4,128)S(1)}, f32[4,416]{1,0:T(4,128)}, u32[]{:S(2)}) copy-start(f32[4,416]{1,0:T(4,128)} %param.15) | copy-start | bytes 19972
  76.5 419.5 %copy-start.6 = (f32[4,416]{1,0:T(4,128)S(1)}, f32[4,416]{1,0:T(4,128)}, u32[]{:S(2)}) copy-start(f32[4,416]{1,0:T(4,128)} %param.16) | copy-start | bytes 19972
  76.5 419.5 %copy-start.7 = (f32[4,416]{1,0:T(4,128)S(1)}, f32[4,416]{1,0:T(4,128)}, u32[]{:S(2)}) copy-start(f32[4,416]{1,0:T(4,128)} %param.17) | copy-start | bytes 19972
  76.5 462.3 %all-gather.2.cloned.1.call-start = ((), (), s32[]{:S(2)}) async-start(), calls=%async_computation.3 | async-start | bytes 1253376 | tf_op jit(solution)/shard_map/all_gather | solution.py:45
  538.8 2.3 copy-start
Sparse Core Ops, SparseCore 0:
  10.8 65.6 reduce-scatter.1
  79.4 55.1 all-reduce.1
  495.9 42.8 all-gather.1
where the time goes:
time: 549 us
  blocking collectives  413 us (75%)
  waiting for transfers between devices  108 us (20%)
  between operations  15.9 us (3%)
  other arithmetic  5.98 us (1%)
  local copies, waits for them, and re-layouts  5.74 us (1%)
    psum x1, blocking collectives, body(): lax.psum(jnp.sum(proj_avg * proj_avg) + conv_share, ('dp', 'tensor'))  271 us
    psum x1, blocking collectives, body(): conv_avg = lax.psum(grad_conv[0], ('rep', 'dp')) / replica_count  142 us
    reduce_scatter x1, waiting for transfers between devices, body(): lax.psum_scatter(grad_proj[0], 'dp', scatter_dimension=1, tiled=True)  66.1 us
    all_gather x1, waiting for transfers between devices, body(): lax.all_gather(new_param_proj.astype(jnp.bfloat16), 'dp', axis=1, tiled=T...  42.1 us
  transfers between devices with their start and end apart: 3, of which 2 were waited for; matrix products, arithmetic and copies ran while one was open for 0% of the time, Pallas kernels for 0%

commit v1 on v0

--- a/solution.py
+++ b/solution.py
@@ -8,6 +8,19 @@
 INNER = 3072
 CONV = 3328
 KCONV = 4
+
+
+def ring_gather(x, axis, dim):
+    ways = lax.axis_size(axis)
+    up = [(d, (d + 1) % ways) for d in range(ways)]
+    down = [(d, (d - 1) % ways) for d in range(ways)]
+    earlier, later = ([x], [x])
+    for _ in range(ways // 2):
+        earlier.append(lax.ppermute(earlier[-1], axis, up))
+    for _ in range((ways - 1) // 2):
+        later.append(lax.ppermute(later[-1], axis, down))
+    line = jnp.concatenate([*earlier[::-1], *later[1:]], axis=dim)
+    return jnp.roll(line, (lax.axis_index(axis) - ways // 2) * x.shape[dim], axis=dim)
 
 
 def adamw_step(param_in, first_in, second_in, grad_in):
@@ -42,9 +55,9 @@
         param_conv, m_conv, v_conv, clip_factor * conv_avg
     )
     ema_count = ema_proj.shape[0]
-    full_block = lax.all_gather(
-        new_param_proj.astype(jnp.bfloat16), "dp", axis=1, tiled=True
-    ).astype(new_param_proj.dtype)
+    full_block = ring_gather(new_param_proj.astype(jnp.bfloat16), "dp", 1).astype(
+        new_param_proj.dtype
+    )
     weights_proj = full_block.astype(jnp.bfloat16)
     row_block = lax.dynamic_slice_in_dim(full_block, lax.axis_index("dp") * ema_count, ema_count, 0)
     new_ema_proj = 0.9 * ema_proj + 0.1 * row_block

time: 549 us -> 561 us (1.022)
  starting transfers between devices: 0.12 us -> 37.4 us
  waiting for transfers between devices: 108 us -> 76.6 us
    all_gather x1 -> x0, waiting for transfers between devices: 42.1 us -> none  [body(): lax.all_gather(new_param_proj.astype(jnp.bfloat16), 'dp', axis=1, tiled=T...]
    ppermute x0 -> x15, starting transfers between devices: none -> 37.3 us  [the longest x7 37.3 us: ring_gather(): later.append(lax.ppermute(later[-1], axis, down))]
    ppermute x0 -> x15, waiting for transfers between devices: none -> 10.5 us  [the longest x8 9.5 us: ring_gather(): earlier.append(lax.ppermute(earlier[-1], axis, up))]
  transfers between devices with their start and end apart: 3 -> 17, of which waited for: 2 -> 15; matrix products, arithmetic and copies ran while one was open for 0% -> 0% of each run, Pallas kernels for 0% -> 0%
where the time goes in v1:
time: 561 us; the launch traced here: 558 us
  blocking collectives  413 us (74%)
  waiting for transfers between devices  76.6 us (14%)
  starting transfers between devices  37.4 us (7%)
  between operations  16.3 us (3%)
  local copies, waits for them, and re-layouts  9.7 us (2%)
    psum x1, blocking collectives, body(): lax.psum(jnp.sum(proj_avg * proj_avg) + conv_share, ('dp', 'tensor'))  270 us
    psum x1, blocking collectives, body(): conv_avg = lax.psum(grad_conv[0], ('rep', 'dp')) / replica_count  143 us
    reduce_scatter x1, waiting for transfers between devices, body(): lax.psum_scatter(grad_proj[0], 'dp', scatter_dimension=1, tiled=True)  66.1 us
    ppermute x7, starting transfers between devices, ring_gather(): later.append(lax.ppermute(later[-1], axis, down))  37.3 us
  transfers between devices with their start and end apart: 17, of which 15 were waited for; matrix products, arithmetic and copies ran while one was open for 0% of the time, Pallas kernels for 0%

profile of v1, /device:TPU:1, one launch (start us, length us, event | category | flops | bytes accessed | tf_op | source)
XLA Modules:
  0.0 558.2 jit_solution(11351160351054649460)
XLA Ops:
  7.2 0.0 reduce-scatter.2.cloned.1.call-start
  7.2 3.1 copy.17
  10.3 0.0 copy-start.10
  10.3 0.0 copy-start.11
  10.3 0.0 copy-start.12
  10.3 0.0 reduce-scatter.2.cloned.1.call-update
  10.4 0.0 all-reduce.2.cloned.1.call-start
  10.4 66.1 %reduce-scatter.2.cloned.1.call-done = f32[384,96]{0,1:T(8,128)} async-done(((f32[384,1536]{0,1:T(8,128)}), f32[384,96]{0,1:T(8,128)}) %reduce-scatter.2.cloned.1.call-update) | async-done | bytes 147472 | tf_op jit(solution)/shard_map/reduce_scatter | solution.py:46
  76.5 0.0 all-reduce.2.cloned.1.call-update
  76.5 142.5 %psum.22 = f32[4,416]{1,0:T(4,128)S(1)} all-reduce(f32[4,416]{1,0:T(4,128)S(1)} %bitcast.3), channel_id=1, replica_groups=mesh['rep'=4,'dp'=16,'tensor'=8] {'rep','dp'}, use_global_device_ids=true, to_apply=%region_3.0 | all-reduce | flops 1664 | bytes 13312 | tf_op jit(solution)/shard_map/psum | solution.py:43
  219.1 0.6 multiply_reduce_fusion.1
  220.3 0.0 all-reduce.2.cloned.1.call-done
  220.3 1.6 multiply_reduce_fusion
  222.5 270.5 %psum.23 = f32[]{:T(128)} all-reduce(f32[]{:T(128)S(6)} %add.61), channel_id=1, replica_groups=mesh['rep'=4,'dp'=16,'tensor'=8] {'dp','tensor'}, use_global_device_ids=true, to_apply=%region_5.6 | all-reduce | flops 1 | bytes 8 | tf_op jit(solution)/shard_map/psum | solution.py:49
  493.8 1.7 multiply_subtract_fusion
  495.5 0.1 copy.18
  495.7 0.0 collective-permute-start
  495.7 11.4 %collective-permute-start.8 = (bf16[384,96]{1,0:T(8,128)(2,1)S(1)}, bf16[384,96]{1,0:T(8,128)(2,1)S(1)}, u32[]{:S(2)}, u32[]{:S(2)}) collective-permute-start(bf16[384,96]{1,0:T(8,128)(2,1)S(1)} %copy.18), channel_id=1, source_target_pairs={{0,120},{8,0},{16,8},{24,16},{32,24},{40,32},{48,40},{56,48},{64,5... | collective-permute-start | bytes 221192 | tf_op jit(solution)/shard_map/ppermute | solution.py:21
  507.1 0.8 collective-permute-done
  507.9 0.0 collective-permute-start.1
  507.9 0.2 collective-permute-done.8
  508.0 4.3 collective-permute-start.9
  512.3 0.8 collective-permute-done.1
  513.1 0.0 collective-permute-start.2
  513.1 0.2 collective-permute-done.9
  513.3 4.3 collective-permute-start.10
  517.6 0.8 collective-permute-done.2
  518.4 0.0 collective-permute-start.3
  518.4 0.2 collective-permute-done.10
  518.5 4.3 collective-permute-start.11
  522.8 0.8 collective-permute-done.3
  523.6 0.0 collective-permute-start.4
  523.6 0.2 collective-permute-done.11
  523.8 4.3 collective-permute-start.12
  528.1 0.8 collective-permute-done.4
  528.9 0.2 collective-permute-done.12
  529.0 4.3 collective-permute-start.13
  533.4 0.8 collective-permute-done.5
  534.1 0.2 collective-permute-done.13
  534.3 4.3 collective-permute-start.14
  538.6 0.8 collective-permute-done.6
  539.4 0.6 multiply_subtract_fusion.1
  540.1 0.6 copy-done.5
  540.7 4.0 collective-permute-done.7
  544.8 4.2 concatenate.6
  549.0 0.0 copy-start.9
  549.1 1.6 constant_dynamic-slice_fusion
  550.6 0.8 multiply_add_fusion
  (27 shorter events, 0.1 us)
Async XLA Ops:
  7.2 69.3 %reduce-scatter.2.cloned.1.call-start = ((), (), s32[]{:S(2)}) async-start(), calls=%async_computation.1 | async-start | bytes 2506752 | tf_op jit(solution)/shard_map/reduce_scatter | solution.py:46
  10.3 66.2 %copy-start.13 = (f32[1,4,416]{2,1,0:T(4,128)S(1)}, f32[1,4,416]{2,1,0:T(4,128)}, u32[]{:S(2)}) copy-start(f32[1,4,416]{2,1,0:T(4,128)} %param.10) | copy-start | bytes 19972
  10.3 483.5 %copy-start.6 = (f32[384,96]{0,1:T(8,128)S(1)}, f32[384,96]{0,1:T(8,128)}, u32[]{:S(2)}) copy-start(f32[384,96]{0,1:T(8,128)} %param.11) | copy-start | bytes 442372
  10.3 483.5 %copy-start.7 = (f32[384,96]{0,1:T(8,128)S(1)}, f32[384,96]{0,1:T(8,128)}, u32[]{:S(2)}) copy-start(f32[384,96]{0,1:T(8,128)} %param.12) | copy-start | bytes 442372
  10.3 483.5 %copy-start.8 = (f32[384,96]{0,1:T(8,128)S(1)}, f32[384,96]{0,1:T(8,128)}, u32[]{:S(2)}) copy-start(f32[384,96]{0,1:T(8,128)} %param.13) | copy-start | bytes 442372
  10.3 529.1 %copy-start.10 = (f32[4,416]{1,0:T(4,128)S(1)}, f32[4,416]{1,0:T(4,128)}, u32[]{:S(2)}) copy-start(f32[4,416]{1,0:T(4,128)} %param.15) | copy-start | bytes 19972
  10.3 529.1 %copy-start.11 = (f32[4,416]{1,0:T(4,128)S(1)}, f32[4,416]{1,0:T(4,128)}, u32[]{:S(2)}) copy-start(f32[4,416]{1,0:T(4,128)} %param.16) | copy-start | bytes 19972
  10.3 529.1 %copy-start.12 = (f32[4,416]{1,0:T(4,128)S(1)}, f32[4,416]{1,0:T(4,128)}, u32[]{:S(2)}) copy-start(f32[4,416]{1,0:T(4,128)} %param.17) | copy-start | bytes 19972
  10.4 210.0 %all-reduce.2.cloned.1.call-start = ((), (), s32[]{:S(2)}) async-start(), calls=%async_computation.2 | async-start | bytes 294912 | tf_op jit(solution)/shard_map/psum | solution.py:47
  495.5 53.5 %copy-start = (f32[384,96]{0,1:T(8,128)}, f32[384,96]{0,1:T(8,128)S(1)}, u32[]{:S(2)}) copy-start(f32[384,96]{0,1:T(8,128)S(1)} %get-tuple-element.11) | copy-start | bytes 442372
  495.7 12.2 %collective-permute-start = (bf16[384,96]{1,0:T(8,128)(2,1)S(1)}, bf16[384,96]{1,0:T(8,128)(2,1)S(1)}, u32[]{:S(2)}, u32[]{:S(2)}) collective-permute-start(bf16[384,96]{1,0:T(8,128)(2,1)S(1)} %copy.18), channel_id=1, source_target_pairs={{0,8},{8,16},{16,24},{24,32},{32,40},{40,48},{48,56},{56,64},{64,7... | collective-permute-start | bytes 221192 | tf_op jit(solution)/shard_map/ppermute | solution.py:19
  495.7 12.4 %collective-permute-start.8 = (bf16[384,96]{1,0:T(8,128)(2,1)S(1)}, bf16[384,96]{1,0:T(8,128)(2,1)S(1)}, u32[]{:S(2)}, u32[]{:S(2)}) collective-permute-start(bf16[384,96]{1,0:T(8,128)(2,1)S(1)} %copy.18), channel_id=1, source_target_pairs={{0,120},{8,0},{16,8},{24,16},{32,24},{40,32},{48,40},{56,48},{64,5... | collective-permute-start | bytes 221192 | tf_op jit(solution)/shard_map/ppermute | solution.py:21
  507.9 5.2 collective-permute-start.1
  508.0 5.2 collective-permute-start.9
  513.1 5.3 collective-permute-start.2
  513.3 5.3 collective-permute-start.10
  518.4 5.3 collective-permute-start.3
  518.5 5.3 collective-permute-start.11
  523.6 5.3 collective-permute-start.4
  523.8 5.3 collective-permute-start.12
  528.9 5.3 collective-permute-start.5
  529.0 11.0 %copy-start.1 = (bf16[384,96]{1,0:T(8,128)(2,1)}, bf16[384,96]{1,0:T(8,128)(2,1)S(1)}, u32[]{:S(2)}) copy-start(bf16[384,96]{1,0:T(8,128)(2,1)S(1)} %collective-permute-done.12) | copy-start | bytes 221188
  529.0 5.3 collective-permute-start.13
  534.1 5.9 %copy-start.2 = (bf16[384,96]{1,0:T(8,128)(2,1)}, bf16[384,96]{1,0:T(8,128)(2,1)S(1)}, u32[]{:S(2)}) copy-start(bf16[384,96]{1,0:T(8,128)(2,1)S(1)} %collective-permute-done.5) | copy-start | bytes 221188
  534.1 5.3 collective-permute-start.6
  534.3 5.8 %copy-start.3 = (bf16[384,96]{1,0:T(8,128)(2,1)}, bf16[384,96]{1,0:T(8,128)(2,1)S(1)}, u32[]{:S(2)}) copy-start(bf16[384,96]{1,0:T(8,128)(2,1)S(1)} %collective-permute-done.13) | copy-start | bytes 221188
  534.3 5.8 %collective-permute-start.14 = (bf16[384,96]{1,0:T(8,128)(2,1)S(1)}, bf16[384,96]{1,0:T(8,128)(2,1)S(1)}, u32[]{:S(2)}, u32[]{:S(2)}) collective-permute-start(bf16[384,96]{1,0:T(8,128)(2,1)S(1)} %collective-permute-done.13), channel_id=1, source_target_pairs={{0,120},{8,0},{16,8},{24,16},{32,24},{40,32},{48,40},{56,48},{64,5... | collective-permute-start | bytes 221192 | tf_op jit(solution)/shard_map/ppermute | solution.py:21
  539.4 0.7 copy-start.4
  539.4 5.4 collective-permute-start.7
  540.1 0.6 copy-start.5
  549.0 1.6 copy-start.9
Sparse Core Ops, SparseCore 0:
  10.8 65.6 reduce-scatter.1
  79.4 54.9 all-reduce.1
